TPU v7x, 32 devices: a whole 2x2x4 slice. The times are simulated.
32 devices in a mesh: blk: 8 (over z, x), grp: 4 (over y, core).
Axes of the slice: x: 2, y: 2, z: 4, core: 2. Of those that a mesh axis runs over, the one named last changes fastest.
Arguments:
- image_student: bfloat16 [8, 4, 256, 768], P('blk', 'grp'), may hold values from -6 to 6
- image_teacher: bfloat16 [8, 4, 256, 1152], P('blk', 'grp'), may hold values from -6 to 6
- text_student: bfloat16 [8, 4, 256, 768], P('blk', 'grp'), may hold values from -6 to 6
- text_teacher: bfloat16 [8, 4, 256, 1152], P('blk', 'grp'), may hold values from -6 to 6
- pair_ids: int32 [8, 4, 256], P('blk', 'grp'), may hold values from 0 to 511
Outputs:
- image_grad: float32 [8, 4, 256, 768], P('blk', 'grp')
- text_grad: float32 [8, 4, 256, 768], P('blk', 'grp')
- bias_grad: float32 [], replicated
All inputs are finite; a program needn't handle non-finite values.
Results may differ from a plain program's by a relative error of at most 0.0021.
Values may be sent and summed in bfloat16 or wider, within the bound.
A program may use at most 64 MiB of HBM per device.

v0:
```python
import functools
import math

import jax
import jax.numpy as jnp
from jax import lax
from jax.experimental import pallas as pl
from jax.experimental.pallas import tpu as pltpu
from jax.sharding import PartitionSpec as P

MESH = pl.DeviceIdType.MESH
WINDOW = 4
F_CHUNKS = 4
N_CHUNKS = 4
OUT_CHUNKS = 4


def dot_nt(a, b):
    return lax.dot_general(a, b, (((1,), (1,)), ((), ())), preferred_element_type=jnp.float32)


def dot_tn(a, b):
    return lax.dot_general(a, b, (((0,), (0,)), ((), ())), preferred_element_type=jnp.float32)


def dot_nn(a, b):
    return jnp.dot(a, b, preferred_element_type=jnp.float32)


def fold(w):
    w = jnp.sum(w.reshape(w.shape[0] // 8, 8, w.shape[1]), axis=0)
    out = w[:, 0:128]
    for at in range(128, w.shape[1], 128):
        out = out + w[:, at : at + 128]
    return out


def kernel(
    n_blk,
    n_grp,
    ds,
    inv_count,
    img_stu,
    img_tea,
    txt_stu,
    txt_tea,
    ids,
    out_img,
    out_txt,
    out_bias,
    far,
    near,
    own_ids,
    far_in,
    near_in,
    far_ids_in,
    near_ids_in,
    acc_far,
    acc_near,
    acc_pn,
    pf_out,
    pn_out,
    pf_in,
    pn_in,
    total,
    stage1_own,
    stage1,
    stage2_own,
    stage2,
    local_sem,
    far_send,
    far_recv,
    near_send,
    near_recv,
    ids_send,
    ids_recv,
    pf_send,
    pf_recv,
    pn_send,
    pn_recv,
    s1_send,
    s1_recv,
    s2_send,
    s2_recv,
    out_sem,
):
    b = lax.axis_index("blk")
    g = lax.axis_index("grp")
    size = far.shape[0]
    dt = far.shape[1] - ds
    role = lax.rem(g, 2)
    step = 1 - 2 * role
    far_to = lax.rem(b + 2 * step + 2 * n_blk, n_blk)
    far_from = lax.rem(b - 2 * step + 2 * n_blk, n_blk)
    near_to = lax.rem(b - step + n_blk, n_blk)
    near_from = lax.rem(b + step + n_blk, n_blk)

    def at_blk(i):
        return {"blk": i, "grp": g}

    def loads(f_stu, f_tea, n_stu, n_tea):
        return [
            pltpu.make_async_copy(f_stu, far.at[:, pl.ds(0, ds)], local_sem.at[0]),
            pltpu.make_async_copy(f_tea, far.at[:, pl.ds(ds, dt)], local_sem.at[1]),
            pltpu.make_async_copy(n_stu, near.at[:, pl.ds(0, ds)], local_sem.at[2]),
            pltpu.make_async_copy(n_tea, near.at[:, pl.ds(ds, dt)], local_sem.at[3]),
        ]

    @pl.when(role == 0)
    def _():
        for c in loads(txt_stu, txt_tea, img_stu, img_tea):
            c.start()

    @pl.when(role == 1)
    def _():
        for c in loads(img_stu, img_tea, txt_stu, txt_tea):
            c.start()

    ids_load = pltpu.make_async_copy(ids, own_ids, local_sem.at[4])
    ids_load.start()

    barrier = pltpu.get_barrier_semaphore()
    for k in range(1, n_blk):
        pl.semaphore_signal(
            barrier, inc=1, device_id=at_blk(lax.rem(b + k, n_blk)), device_id_type=MESH
        )
    for k in range(1, n_grp):
        pl.semaphore_signal(
            barrier,
            inc=1,
            device_id={"blk": b, "grp": lax.rem(g + k, n_grp)},
            device_id_type=MESH,
        )
    for c in loads(txt_stu, txt_tea, img_stu, img_tea):
        c.wait()
    ids_load.wait()
    pl.semaphore_wait(barrier, n_blk - 1 + n_grp - 1)

    def remote(src, dst, send, recv, to):
        return pltpu.make_async_remote_copy(
            src_ref=src, dst_ref=dst, send_sem=send, recv_sem=recv,
            device_id=to, device_id_type=MESH,
        )

    fr = size // F_CHUNKS
    nr = size // N_CHUNKS
    ids_f = remote(own_ids, far_ids_in, ids_send.at[0], ids_recv.at[0], at_blk(far_to))
    ids_n = remote(own_ids, near_ids_in, ids_send.at[1], ids_recv.at[1], at_blk(near_to))
    ids_n.start()
    ids_f.start()
    near_copies = [
        remote(
            near.at[pl.ds(j * nr, nr)], near_in.at[pl.ds(j * nr, nr)],
            near_send.at[j], near_recv.at[j], at_blk(near_to),
        )
        for j in range(N_CHUNKS)
    ]
    far_copies = [
        remote(
            far.at[pl.ds(i * fr, fr)], far_in.at[pl.ds(i * fr, fr)],
            far_send.at[i], far_recv.at[i], at_blk(far_to),
        )
        for i in range(F_CHUNKS)
    ]
    for c in near_copies:
        c.start()
    for c in far_copies:
        c.start()

    scale_s = 2.0 / math.sqrt(ds)
    scale_t = 2.0 / math.sqrt(dt)

    def as_column(row):
        return jnp.transpose(jnp.broadcast_to(row, (128, row.shape[1])))[:, 0:1]

    def weigh(f, n, f_id, n_id):
        s = dot_nt(f[:, :ds], n[:, :ds]) * (0.5 * scale_s) - 0.5
        q = dot_nt(f[:, ds:], n[:, ds:]) * (0.5 * scale_t) - 0.5
        shift = jnp.where(f_id == n_id, -0.25, 0.25)
        return 0.5 * jnp.tanh(s) - 0.25 * jnp.tanh(q) + shift

    own_row = own_ids[...]
    own_col = as_column(own_row)

    w = weigh(far[...], near[...], own_col, own_row)
    total[...] = fold(w)
    wb = w.astype(jnp.bfloat16)
    acc_far[...] = dot_nn(wb, near[:, :ds])
    acc_near[...] = dot_tn(wb, far[:, :ds])

    ids_n.wait_recv()
    near_row = near_ids_in[...]
    for j in range(N_CHUNKS):
        near_copies[j].wait_recv()
        rows = pl.ds(j * nr, nr)
        w = weigh(near_in[rows, :], far[...], as_column(near_row)[j * nr : (j + 1) * nr], own_row)
        total[...] += fold(w)
        wb = w.astype(jnp.bfloat16)
        acc_far[...] += dot_tn(wb, near_in[rows, pl.ds(0, ds)])
        acc_pn[rows, :] = dot_nn(wb, far[:, :ds])

    def share_total():
        stage1_own[...] = total[...]
        stage1[pl.ds(b, 1)] = total[...][None]
        s1 = []
        for k in range(1, n_blk):
            c = remote(
                stage1_own, stage1.at[b], s1_send.at[k - 1], s1_recv.at[k - 1],
                at_blk(lax.rem(b + k, n_blk)),
            )
            c.start()
            s1.append(c)
        return s1

    ids_f.wait_recv()
    far_col = as_column(far_ids_in[...])
    pf_copies = []
    for i in range(F_CHUNKS):
        far_copies[i].wait_recv()
        rows = pl.ds(i * fr, fr)
        f = far_in[rows, :]
        f_id = far_col[i * fr : (i + 1) * fr]
        w1 = weigh(f, near[...], f_id, own_row)
        w2 = weigh(f, near_in[...], f_id, near_row)
        total[...] += fold(w1) + fold(w2)
        if i == F_CHUNKS - 1:
            s1 = share_total()
        w1 = w1.astype(jnp.bfloat16)
        w2 = w2.astype(jnp.bfloat16)
        back = dot_nn(w1, near[:, :ds]) + dot_nn(w2, near_in[:, :ds])
        pf_out[rows, :] = (back * scale_s).astype(jnp.bfloat16)
        c = remote(
            pf_out.at[rows], pf_in.at[rows], pf_send.at[i], pf_recv.at[i], at_blk(far_from)
        )
        c.start()
        pf_copies.append(c)
        acc_near[...] += dot_tn(w1, f[:, :ds])
        acc_pn[...] += dot_tn(w2, f[:, :ds])

    pr = size // OUT_CHUNKS
    pn_copies = []
    for j in range(OUT_CHUNKS):
        rows = pl.ds(j * pr, pr)
        pn_out[rows, :] = (acc_pn[rows, :] * scale_s).astype(jnp.bfloat16)
        c = remote(
            pn_out.at[rows], pn_in.at[rows], pn_send.at[j], pn_recv.at[j], at_blk(near_from)
        )
        c.start()
        pn_copies.append(c)

    for c in s1:
        c.wait_recv()
    part = stage1[0]
    for k in range(1, n_blk):
        part = part + stage1[k]
    stage2_own[...] = part
    stage2[pl.ds(g, 1)] = part[None]
    s2 = []
    for k in range(1, n_grp):
        c = remote(
            stage2_own, stage2.at[g], s2_send.at[k - 1], s2_recv.at[k - 1],
            {"blk": b, "grp": lax.rem(g + k, n_grp)},
        )
        c.start()
        s2.append(c)

    written = []

    def finish(copies, acc, arrived, rows_each, out_a, out_b, first):
        for i, c in enumerate(copies):
            c.wait_recv()
            rows = pl.ds(i * rows_each, rows_each)
            acc[rows, :] = acc[rows, :] * scale_s + arrived[rows, :].astype(jnp.float32)
            put_a = pltpu.make_async_copy(acc.at[rows], out_a.at[rows], out_sem.at[first + i])
            put_b = pltpu.make_async_copy(acc.at[rows], out_b.at[rows], out_sem.at[first + i])
            written.append(put_a)

            @pl.when(role == 0)
            def _():
                put_a.start()

            @pl.when(role == 1)
            def _():
                put_b.start()

    finish(pf_copies, acc_far, pf_in, fr, out_txt, out_img, 0)
    finish(pn_copies, acc_near, pn_in, pr, out_img, out_txt, F_CHUNKS)

    for c in s2:
        c.wait_recv()
    whole = stage2[0]
    for k in range(1, n_grp):
        whole = whole + stage2[k]
    out_bias[0, 0] = jnp.sum(whole) * inv_count

    for c in written:
        c.wait()
    for c in [ids_f, ids_n] + near_copies + far_copies + pf_copies + pn_copies + s1 + s2:
        c.wait_send()


def land(a, b, out_a, out_b, held, came, went):
    each = a.shape[0] // OUT_CHUNKS
    pieces = [(at, i) for i in range(OUT_CHUNKS) for at in range(2)]
    arrays = ((a, out_a), (b, out_b))
    ins, outs = [], []
    for at, i in pieces:
        rows = pl.ds(i * each, each)
        src, dst = arrays[at]
        ins.append(pltpu.make_async_copy(src.at[rows], held.at[at, rows], came.at[at, i]))
        outs.append(pltpu.make_async_copy(held.at[at, rows], dst.at[rows], went.at[at, i]))
    for c in ins:
        c.start()
    for c, d in zip(ins, outs):
        c.wait()
        d.start()
    for d in outs:
        d.wait()


def solution(mesh):
    n_blk, n_grp = mesh.shape["blk"], mesh.shape["grp"]

    def body(image_student, image_teacher, text_student, text_teacher, pair_ids):
        size, ds = image_student.shape[2:]
        dt = image_teacher.shape[3]
        bf, f32 = jnp.bfloat16, jnp.float32
        dma = lambda k: pltpu.SemaphoreType.DMA((max(k, 1),))
        count = float(n_blk * n_grp * WINDOW * size * size)
        img, txt, bias = pl.pallas_call(
            functools.partial(kernel, n_blk, n_grp, ds, 1.0 / count),
            out_shape=(
                jax.ShapeDtypeStruct((size, ds), f32),
                jax.ShapeDtypeStruct((size, ds), f32),
                jax.ShapeDtypeStruct((1, 1), f32),
            ),
            in_specs=[pl.BlockSpec(memory_space=pl.ANY)] * 5,
            out_specs=(
                pl.BlockSpec(memory_space=pl.ANY),
                pl.BlockSpec(memory_space=pl.ANY),
                pl.BlockSpec(memory_space=pltpu.SMEM),
            ),
            scratch_shapes=[
                pltpu.VMEM((size, ds + dt), bf),
                pltpu.VMEM((size, ds + dt), bf),
                pltpu.VMEM((1, size), jnp.int32),
                pltpu.VMEM((size, ds + dt), bf),
                pltpu.VMEM((size, ds + dt), bf),
                pltpu.VMEM((1, size), jnp.int32),
                pltpu.VMEM((1, size), jnp.int32),
                pltpu.VMEM((size, ds), f32),
                pltpu.VMEM((size, ds), f32),
                pltpu.VMEM((size, ds), f32),
                pltpu.VMEM((size, ds), bf),
                pltpu.VMEM((size, ds), bf),
                pltpu.VMEM((size, ds), bf),
                pltpu.VMEM((size, ds), bf),
                pltpu.VMEM((8, 128), f32),
                pltpu.VMEM((8, 128), f32),
                pltpu.VMEM((n_blk, 8, 128), f32),
                pltpu.VMEM((8, 128), f32),
                pltpu.VMEM((n_grp, 8, 128), f32),
                dma(5),
                dma(F_CHUNKS),
                dma(F_CHUNKS),
                dma(N_CHUNKS),
                dma(N_CHUNKS),
                dma(2),
                dma(2),
                dma(F_CHUNKS),
                dma(F_CHUNKS),
                dma(OUT_CHUNKS),
                dma(OUT_CHUNKS),
                dma(n_blk - 1),
                dma(n_blk - 1),
                dma(n_grp - 1),
                dma(n_grp - 1),
                dma(F_CHUNKS + OUT_CHUNKS),
            ],
            compiler_params=pltpu.CompilerParams(
                collective_id=0, has_side_effects=True, vmem_limit_bytes=62 * 1024 * 1024
            ),
        )(
            image_student[0, 0],
            image_teacher[0, 0],
            text_student[0, 0],
            text_teacher[0, 0],
            pair_ids[0],
        )
        img, txt = pl.pallas_call(
            land,
            out_shape=(
                jax.ShapeDtypeStruct((size, ds), f32),
                jax.ShapeDtypeStruct((size, ds), f32),
            ),
            in_specs=[pl.BlockSpec(memory_space=pl.ANY)] * 2,
            out_specs=[pl.BlockSpec(memory_space=pl.ANY)] * 2,
            scratch_shapes=[
                pltpu.VMEM((2, size, ds), f32),
                pltpu.SemaphoreType.DMA((2, OUT_CHUNKS)),
                pltpu.SemaphoreType.DMA((2, OUT_CHUNKS)),
            ],
            compiler_params=pltpu.CompilerParams(vmem_limit_bytes=62 * 1024 * 1024),
        )(img, txt)
        return img[None, None], txt[None, None], bias[0, 0]

    return jax.shard_map(
        body,
        mesh=mesh,
        in_specs=(
            P("blk", "grp", None, None),
            P("blk", "grp", None, None),
            P("blk", "grp", None, None),
            P("blk", "grp", None, None),
            P("blk", "grp", None),
        ),
        out_specs=(P("blk", "grp", None, None), P("blk", "grp", None, None), P()),
        check_vma=False,
    )
```

profile of v0, /device:TPU:2, one launch (start us, length us, event | category | flops | bytes accessed | tf_op | source)
XLA Modules:
  0.0 60.5 jit_solution(15344508574759662210)
XLA Ops:
  0.6 55.8 %shard_map.76 = (f32[256,768]{1,0:T(8,128)}, f32[256,768]{1,0:T(8,128)}, f32[1,1]{1,0:T(1,128)}) custom-call(bf16[256,768]{1,0:T(8,128)(2,1)} %bitcast.10, bf16[256,1152]{1,0:T(8,128)(2,1)} %bitcast.8, bf16[256,768]{1,0:T(8,128)(2,1)} %bitcast.11, bf16[256,1152]{1,0:T(8,128)(2,1)} %bitcast.9, s32[1,256]{1,0:T(1,128)} %bitcast.12), custom_call_target="tpu_custom_call" | custom-call | tf_op jit(solution)/shard_map/pallas_call | solution.py:330
  56.4 2.3 %shard_map.77 = (f32[256,768]{1,0:T(8,128)}, f32[256,768]{1,0:T(8,128)}) custom-call(f32[256,768]{1,0:T(8,128)} %get-tuple-element.8.a, f32[256,768]{1,0:T(8,128)} %get-tuple-element.9.b), custom_call_target="tpu_custom_call" | custom-call | tf_op jit(solution)/shard_map/pallas_call | solution.py:390
where the time goes:
time: 60.6 us; the launch traced here: 60.5 us
  Pallas kernels  58.1 us (96%)
  between operations  2.41 us (4%)
    pallas_call x1, Pallas kernels, body(): pl.pallas_call(functools.partial(kernel, n_blk, n_grp, ds, 1.0 / count),...  55.8 us
    pallas_call x1, Pallas kernels, body(): pl.pallas_call(land, out_shape=(jax.ShapeDtypeStruct((size, ds), f32), ja...  2.29 us

commit v1 on v0

v1 whole, which is shorter than its diff:
```python
import functools
import math

import jax
import jax.numpy as jnp
from jax import lax
from jax.experimental import pallas as pl
from jax.experimental.pallas import tpu as pltpu
from jax.sharding import PartitionSpec as P

MESH = pl.DeviceIdType.MESH
WINDOW = 4
CHUNKS = 4
PLAIN = ("nnnnffff", "")
NEAR_WRAPS = ("ffff", "nnnn")
FAR_WRAPS = ("nnnn", "ffff")


def dot_nt(a, b):
    return lax.dot_general(a, b, (((1,), (1,)), ((), ())), preferred_element_type=jnp.float32)


def dot_tn(a, b):
    return lax.dot_general(a, b, (((0,), (0,)), ((), ())), preferred_element_type=jnp.float32)


def dot_nn(a, b):
    return jnp.dot(a, b, preferred_element_type=jnp.float32)


def fold(w):
    w = jnp.sum(w.reshape(w.shape[0] // 8, 8, w.shape[1]), axis=0)
    out = w[:, 0:128]
    for at in range(128, w.shape[1], 128):
        out = out + w[:, at : at + 128]
    return out


def kernel(
    n_blk,
    n_grp,
    ds,
    inv_count,
    img_stu,
    img_tea,
    txt_stu,
    txt_tea,
    ids,
    acc_far,
    acc_near,
    out_bias,
    far,
    near,
    own_ids,
    far_in,
    near_in,
    far_ids_in,
    near_ids_in,
    part,
    pf_out,
    pn_out,
    pf_in,
    pn_in,
    total,
    stage1_own,
    stage1,
    stage2_own,
    stage2,
    local_sem,
    far_send,
    far_recv,
    near_send,
    near_recv,
    ids_send,
    ids_recv,
    pf_send,
    pf_recv,
    pn_send,
    pn_recv,
    s1_send,
    s1_recv,
    s2_send,
    s2_recv,
    up_sem,
    down_sem,
):
    b = lax.axis_index("blk")
    g = lax.axis_index("grp")
    size = far.shape[0]
    dt = far.shape[1] - ds
    role = lax.rem(g, 2)
    step = 1 - 2 * role
    far_to = lax.rem(b + 2 * step + 2 * n_blk, n_blk)
    far_from = lax.rem(b - 2 * step + 2 * n_blk, n_blk)
    near_to = lax.rem(b - step + n_blk, n_blk)
    near_from = lax.rem(b + step + n_blk, n_blk)

    def at_blk(i):
        return {"blk": i, "grp": g}

    def loads(f_stu, f_tea, n_stu, n_tea):
        return [
            pltpu.make_async_copy(f_stu, far.at[:, pl.ds(0, ds)], local_sem.at[0]),
            pltpu.make_async_copy(f_tea, far.at[:, pl.ds(ds, dt)], local_sem.at[1]),
            pltpu.make_async_copy(n_stu, near.at[:, pl.ds(0, ds)], local_sem.at[2]),
            pltpu.make_async_copy(n_tea, near.at[:, pl.ds(ds, dt)], local_sem.at[3]),
        ]

    @pl.when(role == 0)
    def _():
        for c in loads(txt_stu, txt_tea, img_stu, img_tea):
            c.start()

    @pl.when(role == 1)
    def _():
        for c in loads(img_stu, img_tea, txt_stu, txt_tea):
            c.start()

    ids_load = pltpu.make_async_copy(ids, own_ids, local_sem.at[4])
    ids_load.start()

    has_up, has_down = b + 2 < n_blk, b >= 2
    links = ((1, b + 1 < n_blk), (2, has_up), (-1, b >= 1), (-2, has_down))
    barrier = pltpu.get_barrier_semaphore()
    expected = jnp.int32(n_grp - 1)
    for offset, present in links:
        expected = expected + present.astype(jnp.int32)

        @pl.when(present)
        def _():
            pl.semaphore_signal(
                barrier, inc=1, device_id=at_blk(b + offset), device_id_type=MESH
            )

    for k in range(1, n_grp):
        pl.semaphore_signal(
            barrier,
            inc=1,
            device_id={"blk": b, "grp": lax.rem(g + k, n_grp)},
            device_id_type=MESH,
        )
    for c in loads(txt_stu, txt_tea, img_stu, img_tea):
        c.wait()
    ids_load.wait()
    pl.semaphore_wait(barrier, expected)

    def remote(src, dst, send, recv, to):
        return pltpu.make_async_remote_copy(
            src_ref=src, dst_ref=dst, send_sem=send, recv_sem=recv,
            device_id=to, device_id_type=MESH,
        )

    each = size // CHUNKS
    ids_f = remote(own_ids, far_ids_in, ids_send.at[0], ids_recv.at[0], at_blk(far_to))
    ids_n = remote(own_ids, near_ids_in, ids_send.at[1], ids_recv.at[1], at_blk(near_to))
    near_copies = [
        remote(
            near.at[pl.ds(j * each, each)], near_in.at[pl.ds(j * each, each)],
            near_send.at[j], near_recv.at[j], at_blk(near_to),
        )
        for j in range(CHUNKS)
    ]
    far_copies = [
        remote(
            far.at[pl.ds(i * each, each)], far_in.at[pl.ds(i * each, each)],
            far_send.at[i], far_recv.at[i], at_blk(far_to),
        )
        for i in range(CHUNKS)
    ]
    near_wraps = jnp.where(role == 0, b == 0, b == n_blk - 1)
    far_wraps = jnp.where(role == 0, jnp.logical_not(has_up), jnp.logical_not(has_down))

    def begin(order, done=""):
        sent = {"n": done.count("n"), "f": done.count("f")}
        for kind in order:
            ids_copy, copies = (ids_n, near_copies) if kind == "n" else (ids_f, far_copies)
            if sent[kind] == 0:
                ids_copy.start()
            copies[sent[kind]].start()
            sent[kind] += 1

    plain = jnp.logical_not(jnp.logical_or(near_wraps, far_wraps))
    cases = ((plain, PLAIN), (near_wraps, NEAR_WRAPS), (far_wraps, FAR_WRAPS))
    for case, (at_once, _) in cases:

        @pl.when(case)
        def _():
            begin(at_once)

    def tell(sem, offset):
        pl.semaphore_signal(sem, inc=1, device_id=at_blk(b + offset), device_id_type=MESH)

    def pass_up():
        @pl.when(has_down)
        def _():
            pl.semaphore_wait(up_sem, 1)

        @pl.when(has_up)
        def _():
            tell(up_sem, 2)

    def pass_down():
        @pl.when(has_up)
        def _():
            pl.semaphore_wait(down_sem, 1)

        @pl.when(has_down)
        def _():
            tell(down_sem, -2)

    lower = b < n_blk // 2

    @pl.when(lower)
    def _():
        pass_up()
        pass_down()

    @pl.when(jnp.logical_not(lower))
    def _():
        pass_down()
        pass_up()

    for case, (at_once, after) in cases:

        @pl.when(case)
        def _():
            begin(after, at_once)

    scale_s = 2.0 / math.sqrt(ds)
    scale_t = 2.0 / math.sqrt(dt)

    def as_column(row):
        return jnp.transpose(jnp.broadcast_to(row, (128, row.shape[1])))[:, 0:1]

    def weigh(f, n, f_id, n_id):
        s = dot_nt(f[:, :ds], n[:, :ds]) * (0.5 * scale_s) - 0.5
        q = dot_nt(f[:, ds:], n[:, ds:]) * (0.5 * scale_t) - 0.5
        shift = jnp.where(f_id == n_id, -0.25, 0.25)
        return 0.5 * jnp.tanh(s) - 0.25 * jnp.tanh(q) + shift

    own_row = own_ids[...]
    own_col = as_column(own_row)

    w = weigh(far[...], near[...], own_col, own_row)
    total[...] = fold(w)
    wb = w.astype(jnp.bfloat16)
    acc_far[...] = dot_nn(wb, near[:, :ds])
    acc_near[...] = dot_tn(wb, far[:, :ds])

    rows_of = [pl.ds(i * each, each) for i in range(CHUNKS)]
    pf_copies = [
        remote(pf_out.at[rows], pf_in.at[rows], pf_send.at[i], pf_recv.at[i], at_blk(far_from))
        for i, rows in enumerate(rows_of)
    ]
    pn_copies = [
        remote(pn_out.at[rows], pn_in.at[rows], pn_send.at[i], pn_recv.at[i], at_blk(near_from))
        for i, rows in enumerate(rows_of)
    ]
    s1 = [
        remote(
            stage1_own, stage1.at[b], s1_send.at[k - 1], s1_recv.at[k - 1],
            at_blk(lax.rem(b + k, n_blk)),
        )
        for k in range(1, n_blk)
    ]

    def share_total():
        stage1_own[...] = total[...]
        stage1[pl.ds(b, 1)] = total[...][None]
        for c in s1:
            c.start()

    far_side = (far, far_in, ids_f, far_ids_in, far_copies, acc_far, pf_out, pf_copies)
    near_side = (near, near_in, ids_n, near_ids_in, near_copies, acc_near, pn_out, pn_copies)

    def process(early, late):
        e_own, e_in, e_ids, e_ids_in, e_copies, e_acc, e_out, e_back = early
        l_own, l_in, l_ids, l_ids_in, l_copies, l_acc, l_out, l_back = late
        e_ids.wait_recv()
        e_row = e_ids_in[...]
        e_col = as_column(e_row)
        for i, rows in enumerate(rows_of):
            e_copies[i].wait_recv()
            x = e_in[rows, :]
            w = weigh(x, l_own[...], e_col[i * each : (i + 1) * each], own_row)
            total[...] += fold(w)
            w = w.astype(jnp.bfloat16)
            l_acc[...] += dot_tn(w, x[:, :ds])
            part[rows, :] = dot_nn(w, l_own[:, :ds])
        l_ids.wait_recv()
        l_col = as_column(l_ids_in[...])
        for i, rows in enumerate(rows_of):
            l_copies[i].wait_recv()
            x = l_in[rows, :]
            x_id = l_col[i * each : (i + 1) * each]
            w1 = weigh(x, e_own[...], x_id, own_row)
            w2 = weigh(x, e_in[...], x_id, e_row)
            total[...] += fold(w1) + fold(w2)
            if i == CHUNKS - 1:
                share_total()
            w1 = w1.astype(jnp.bfloat16)
            w2 = w2.astype(jnp.bfloat16)
            back = dot_nn(w1, e_own[:, :ds]) + dot_nn(w2, e_in[:, :ds])
            l_out[rows, :] = (back * scale_s).astype(jnp.bfloat16)
            l_back[i].start()
            e_acc[...] += dot_tn(w1, x[:, :ds])
            part[...] += dot_tn(w2, x[:, :ds])
        for i, rows in enumerate(rows_of):
            e_out[rows, :] = (part[rows, :] * scale_s).astype(jnp.bfloat16)
            e_back[i].start()

    process(far_side, near_side)

    def finish(copies, acc, arrived):
        for c, rows in zip(copies, rows_of):
            c.wait_recv()
            acc[rows, :] = acc[rows, :] * scale_s + arrived[rows, :].astype(jnp.float32)

    finish(pn_copies, acc_near, pn_in)
    for c in s1:
        c.wait_recv()
    total_blk = stage1[0]
    for k in range(1, n_blk):
        total_blk = total_blk + stage1[k]
    stage2_own[...] = total_blk
    stage2[pl.ds(g, 1)] = total_blk[None]
    s2 = []
    for k in range(1, n_grp):
        c = remote(
            stage2_own, stage2.at[g], s2_send.at[k - 1], s2_recv.at[k - 1],
            {"blk": b, "grp": lax.rem(g + k, n_grp)},
        )
        c.start()
        s2.append(c)
    finish(pf_copies, acc_far, pf_in)

    for c in s2:
        c.wait_recv()
    whole = stage2[0]
    for k in range(1, n_grp):
        whole = whole + stage2[k]
    out_bias[...] = jnp.full((1, 1), jnp.sum(whole) * inv_count, jnp.float32)

    for c in [ids_f, ids_n] + near_copies + far_copies + pf_copies + pn_copies + s1 + s2:
        c.wait_send()


def land(of_far, of_near, bias, out_img, out_txt, out_bias, sems):
    role = lax.rem(lax.axis_index("grp"), 2)

    def put(a, b):
        return [
            pltpu.make_async_copy(a, out_img, sems.at[0]),
            pltpu.make_async_copy(b, out_txt, sems.at[1]),
        ]

    @pl.when(role == 0)
    def _():
        for c in put(of_near, of_far):
            c.start()

    @pl.when(role == 1)
    def _():
        for c in put(of_far, of_near):
            c.start()

    put_bias = pltpu.make_async_copy(bias, out_bias, sems.at[2])
    put_bias.start()
    put_bias.wait()
    for c in put(of_near, of_far):
        c.wait()


def solution(mesh):
    n_blk, n_grp = mesh.shape["blk"], mesh.shape["grp"]

    def body(image_student, image_teacher, text_student, text_teacher, pair_ids):
        size, ds = image_student.shape[2:]
        dt = image_teacher.shape[3]
        bf, f32 = jnp.bfloat16, jnp.float32
        dma = lambda k: pltpu.SemaphoreType.DMA((max(k, 1),))
        count = float(n_blk * n_grp * WINDOW * size * size)
        far, near, bias = pl.pallas_call(
            functools.partial(kernel, n_blk, n_grp, ds, 1.0 / count),
            out_shape=(
                jax.ShapeDtypeStruct((size, ds), f32),
                jax.ShapeDtypeStruct((size, ds), f32),
                jax.ShapeDtypeStruct((1, 1), f32),
            ),
            in_specs=[pl.BlockSpec(memory_space=pl.ANY)] * 5,
            out_specs=(
                pl.BlockSpec(memory_space=pltpu.VMEM),
                pl.BlockSpec(memory_space=pltpu.VMEM),
                pl.BlockSpec(memory_space=pltpu.VMEM),
            ),
            scratch_shapes=[
                pltpu.VMEM((size, ds + dt), bf),
                pltpu.VMEM((size, ds + dt), bf),
                pltpu.VMEM((1, size), jnp.int32),
                pltpu.VMEM((size, ds + dt), bf),
                pltpu.VMEM((size, ds + dt), bf),
                pltpu.VMEM((1, size), jnp.int32),
                pltpu.VMEM((1, size), jnp.int32),
                pltpu.VMEM((size, ds), f32),
                pltpu.VMEM((size, ds), bf),
                pltpu.VMEM((size, ds), bf),
                pltpu.VMEM((size, ds), bf),
                pltpu.VMEM((size, ds), bf),
                pltpu.VMEM((8, 128), f32),
                pltpu.VMEM((8, 128), f32),
                pltpu.VMEM((n_blk, 8, 128), f32),
                pltpu.VMEM((8, 128), f32),
                pltpu.VMEM((n_grp, 8, 128), f32),
                dma(5),
                dma(CHUNKS),
                dma(CHUNKS),
                dma(CHUNKS),
                dma(CHUNKS),
                dma(2),
                dma(2),
                dma(CHUNKS),
                dma(CHUNKS),
                dma(CHUNKS),
                dma(CHUNKS),
                dma(n_blk - 1),
                dma(n_blk - 1),
                dma(n_grp - 1),
                dma(n_grp - 1),
                pltpu.SemaphoreType.REGULAR,
                pltpu.SemaphoreType.REGULAR,
            ],
            compiler_params=pltpu.CompilerParams(
                collective_id=0, has_side_effects=True, vmem_limit_bytes=30 * 1024 * 1024
            ),
        )(
            *(
                pltpu.with_memory_space_constraint(x, pltpu.HBM)
                for x in (
                    image_student[0, 0],
                    image_teacher[0, 0],
                    text_student[0, 0],
                    text_teacher[0, 0],
                    pair_ids[0],
                )
            )
        )
        img, txt, bias = pl.pallas_call(
            land,
            out_shape=(
                jax.ShapeDtypeStruct((size, ds), f32),
                jax.ShapeDtypeStruct((size, ds), f32),
                jax.ShapeDtypeStruct((1, 1), f32),
            ),
            in_specs=[pl.BlockSpec(memory_space=pltpu.VMEM)] * 3,
            out_specs=[pl.BlockSpec(memory_space=pl.ANY)] * 3,
            scratch_shapes=[dma(3)],
            compiler_params=pltpu.CompilerParams(vmem_limit_bytes=30 * 1024 * 1024),
        )(far, near, bias)
        return img[None, None], txt[None, None], bias[0, 0]

    return jax.shard_map(
        body,
        mesh=mesh,
        in_specs=(
            P("blk", "grp", None, None),
            P("blk", "grp", None, None),
            P("blk", "grp", None, None),
            P("blk", "grp", None, None),
            P("blk", "grp", None),
        ),
        out_specs=(P("blk", "grp", None, None), P("blk", "grp", None, None), P()),
        check_vma=False,
    )
```

time: 60.6 us -> 59.4 us (0.980); the launches traced: 60.5 us -> 58.6 us
  between operations: 2.41 us -> 0.64 us
where the time goes in v1:
time: 59.4 us; the launch traced here: 58.6 us
  Pallas kernels  57.9 us (97%)
  between operations  0.64 us (1%)
    pallas_call x1, Pallas kernels, body(): pl.pallas_call(functools.partial(kernel, n_blk, n_grp, ds, 1.0 / count),...  56.1 us
    pallas_call x1, Pallas kernels, body(): pl.pallas_call(land, out_shape=(jax.ShapeDtypeStruct((size, ds), f32), ja...  1.81 us

profile of v1, /device:TPU:2, one launch (start us, length us, event | category | flops | bytes accessed | tf_op | source)
XLA Modules:
  0.0 58.6 jit_solution(16996188623498239185)
XLA Ops:
  0.6 56.1 %shard_map.76 = (f32[256,768]{1,0:T(8,128)S(1)}, f32[256,768]{1,0:T(8,128)S(1)}, f32[1,1]{1,0:T(1,128)}) custom-call(bf16[256,768]{1,0:T(8,128)(2,1)} %bitcast.10, bf16[256,1152]{1,0:T(8,128)(2,1)} %bitcast.8, bf16[256,768]{1,0:T(8,128)(2,1)} %bitcast.11, bf16[256,1152]{1,0:T(8,128)(2,1)} %bitcast.9, s32[1,256]{1,0:T(1,128)} %bitcast.12), custom_call_target="tpu_custom_call" | custom-call | tf_op jit(solution)/shard_map/pallas_call | solution.py:383
  56.8 1.8 %shard_map.77 = (f32[256,768]{1,0:T(8,128)}, f32[256,768]{1,0:T(8,128)}, f32[1,1]{1,0:T(1,128)}) custom-call(f32[256,768]{1,0:T(8,128)S(1)} %get-tuple-element.9.of_far, f32[256,768]{1,0:T(8,128)S(1)} %get-tuple-element.10.of_near, f32[1,1]{1,0:T(1,128)} %get-tuple-element.11.bias), custom_call_target="tpu_custom_call" | custom-call | tf_op jit(solution)/shard_map/pallas_call | solution.py:447

commit v2 on v1

--- a/solution.py
+++ b/solution.py
@@ -10,10 +10,11 @@
 
 MESH = pl.DeviceIdType.MESH
 WINDOW = 4
-CHUNKS = 4
-PLAIN = ("nnnnffff", "")
-NEAR_WRAPS = ("ffff", "nnnn")
-FAR_WRAPS = ("nnnn", "ffff")
+FAR = 2
+NEAR = 2
+PLAIN = ("nnff", "")
+NEAR_WRAPS = ("ff", "nn")
+FAR_WRAPS = ("", "ffnn")
 
 
 def dot_nt(a, b):
@@ -40,7 +41,6 @@
     n_blk,
     n_grp,
     ds,
-    inv_count,
     img_stu,
     img_tea,
     txt_stu,
@@ -48,7 +48,7 @@
     ids,
     acc_far,
     acc_near,
-    out_bias,
+    out_total,
     far,
     near,
     own_ids,
@@ -150,22 +150,25 @@
             device_id=to, device_id_type=MESH,
         )
 
-    each = size // CHUNKS
+    def pieces(n):
+        return [(pl.ds(i * (size // n), size // n), slice(i * (size // n), (i + 1) * (size // n))) for i in range(n)]
+
+    far_rows, near_rows = pieces(FAR), pieces(NEAR)
     ids_f = remote(own_ids, far_ids_in, ids_send.at[0], ids_recv.at[0], at_blk(far_to))
     ids_n = remote(own_ids, near_ids_in, ids_send.at[1], ids_recv.at[1], at_blk(near_to))
     near_copies = [
         remote(
-            near.at[pl.ds(j * each, each)], near_in.at[pl.ds(j * each, each)],
+            near.at[rows], near_in.at[rows],
             near_send.at[j], near_recv.at[j], at_blk(near_to),
         )
-        for j in range(CHUNKS)
+        for j, (rows, _) in enumerate(near_rows)
     ]
     far_copies = [
         remote(
-            far.at[pl.ds(i * each, each)], far_in.at[pl.ds(i * each, each)],
+            far.at[rows], far_in.at[rows],
             far_send.at[i], far_recv.at[i], at_blk(far_to),
         )
-        for i in range(CHUNKS)
+        for i, (rows, _) in enumerate(far_rows)
     ]
     near_wraps = jnp.where(role == 0, b == 0, b == n_blk - 1)
     far_wraps = jnp.where(role == 0, jnp.logical_not(has_up), jnp.logical_not(has_down))
@@ -247,14 +250,13 @@
     acc_far[...] = dot_nn(wb, near[:, :ds])
     acc_near[...] = dot_tn(wb, far[:, :ds])
 
-    rows_of = [pl.ds(i * each, each) for i in range(CHUNKS)]
     pf_copies = [
         remote(pf_out.at[rows], pf_in.at[rows], pf_send.at[i], pf_recv.at[i], at_blk(far_from))
-        for i, rows in enumerate(rows_of)
+        for i, (rows, _) in enumerate(far_rows)
     ]
     pn_copies = [
         remote(pn_out.at[rows], pn_in.at[rows], pn_send.at[i], pn_recv.at[i], at_blk(near_from))
-        for i, rows in enumerate(rows_of)
+        for i, (rows, _) in enumerate(near_rows)
     ]
     s1 = [
         remote(
@@ -270,33 +272,33 @@
         for c in s1:
             c.start()
 
-    far_side = (far, far_in, ids_f, far_ids_in, far_copies, acc_far, pf_out, pf_copies)
-    near_side = (near, near_in, ids_n, near_ids_in, near_copies, acc_near, pn_out, pn_copies)
+    far_side = (far, far_in, ids_f, far_ids_in, far_copies, acc_far, pf_out, pf_copies, far_rows)
+    near_side = (near, near_in, ids_n, near_ids_in, near_copies, acc_near, pn_out, pn_copies, near_rows)
 
     def process(early, late):
-        e_own, e_in, e_ids, e_ids_in, e_copies, e_acc, e_out, e_back = early
-        l_own, l_in, l_ids, l_ids_in, l_copies, l_acc, l_out, l_back = late
+        e_own, e_in, e_ids, e_ids_in, e_copies, e_acc, e_out, e_back, e_rows = early
+        l_own, l_in, l_ids, l_ids_in, l_copies, l_acc, l_out, l_back, l_rows = late
         e_ids.wait_recv()
         e_row = e_ids_in[...]
         e_col = as_column(e_row)
-        for i, rows in enumerate(rows_of):
+        for i, (rows, span) in enumerate(e_rows):
             e_copies[i].wait_recv()
             x = e_in[rows, :]
-            w = weigh(x, l_own[...], e_col[i * each : (i + 1) * each], own_row)
+            w = weigh(x, l_own[...], e_col[span], own_row)
             total[...] += fold(w)
             w = w.astype(jnp.bfloat16)
             l_acc[...] += dot_tn(w, x[:, :ds])
             part[rows, :] = dot_nn(w, l_own[:, :ds])
         l_ids.wait_recv()
         l_col = as_column(l_ids_in[...])
-        for i, rows in enumerate(rows_of):
+        for i, (rows, span) in enumerate(l_rows):
             l_copies[i].wait_recv()
             x = l_in[rows, :]
-            x_id = l_col[i * each : (i + 1) * each]
+            x_id = l_col[span]
             w1 = weigh(x, e_own[...], x_id, own_row)
             w2 = weigh(x, e_in[...], x_id, e_row)
             total[...] += fold(w1) + fold(w2)
-            if i == CHUNKS - 1:
+            if i == len(l_rows) - 1:
                 share_total()
             w1 = w1.astype(jnp.bfloat16)
             w2 = w2.astype(jnp.bfloat16)
@@ -305,18 +307,17 @@
             l_back[i].start()
             e_acc[...] += dot_tn(w1, x[:, :ds])
             part[...] += dot_tn(w2, x[:, :ds])
-        for i, rows in enumerate(rows_of):
+        for i, (rows, _) in enumerate(e_rows):
             e_out[rows, :] = (part[rows, :] * scale_s).astype(jnp.bfloat16)
             e_back[i].start()
 
     process(far_side, near_side)
 
-    def finish(copies, acc, arrived):
-        for c, rows in zip(copies, rows_of):
+    def finish(copies, acc, arrived, pieces):
+        for c, (rows, _) in zip(copies, pieces):
             c.wait_recv()
             acc[rows, :] = acc[rows, :] * scale_s + arrived[rows, :].astype(jnp.float32)
 
-    finish(pn_copies, acc_near, pn_in)
     for c in s1:
         c.wait_recv()
     total_blk = stage1[0]
@@ -332,20 +333,21 @@
         )
         c.start()
         s2.append(c)
-    finish(pf_copies, acc_far, pf_in)
+    finish(pn_copies, acc_near, pn_in, near_rows)
+    finish(pf_copies, acc_far, pf_in, far_rows)
 
     for c in s2:
         c.wait_recv()
     whole = stage2[0]
     for k in range(1, n_grp):
         whole = whole + stage2[k]
-    out_bias[...] = jnp.full((1, 1), jnp.sum(whole) * inv_count, jnp.float32)
+    out_total[...] = whole
 
     for c in [ids_f, ids_n] + near_copies + far_copies + pf_copies + pn_copies + s1 + s2:
         c.wait_send()
 
 
-def land(of_far, of_near, bias, out_img, out_txt, out_bias, sems):
+def land(inv_count, of_far, of_near, total, out_img, out_txt, out_bias, mean, sems):
     role = lax.rem(lax.axis_index("grp"), 2)
 
     def put(a, b):
@@ -364,7 +366,8 @@
         for c in put(of_far, of_near):
             c.start()
 
-    put_bias = pltpu.make_async_copy(bias, out_bias, sems.at[2])
+    mean[...] = jnp.full((1, 1), jnp.sum(total[...]) * inv_count, jnp.float32)
+    put_bias = pltpu.make_async_copy(mean, out_bias, sems.at[2])
     put_bias.start()
     put_bias.wait()
     for c in put(of_near, of_far):
@@ -380,12 +383,12 @@
         bf, f32 = jnp.bfloat16, jnp.float32
         dma = lambda k: pltpu.SemaphoreType.DMA((max(k, 1),))
         count = float(n_blk * n_grp * WINDOW * size * size)
-        far, near, bias = pl.pallas_call(
-            functools.partial(kernel, n_blk, n_grp, ds, 1.0 / count),
+        far, near, total = pl.pallas_call(
+            functools.partial(kernel, n_blk, n_grp, ds),
             out_shape=(
                 jax.ShapeDtypeStruct((size, ds), f32),
                 jax.ShapeDtypeStruct((size, ds), f32),
-                jax.ShapeDtypeStruct((1, 1), f32),
+                jax.ShapeDtypeStruct((8, 128), f32),
             ),
             in_specs=[pl.BlockSpec(memory_space=pl.ANY)] * 5,
             out_specs=(
@@ -412,16 +415,16 @@
                 pltpu.VMEM((8, 128), f32),
                 pltpu.VMEM((n_grp, 8, 128), f32),
                 dma(5),
-                dma(CHUNKS),
-                dma(CHUNKS),
-                dma(CHUNKS),
-                dma(CHUNKS),
+                dma(FAR),
+                dma(FAR),
+                dma(NEAR),
+                dma(NEAR),
                 dma(2),
                 dma(2),
-                dma(CHUNKS),
-                dma(CHUNKS),
-                dma(CHUNKS),
-                dma(CHUNKS),
+                dma(FAR),
+                dma(FAR),
+                dma(NEAR),
+                dma(NEAR),
                 dma(n_blk - 1),
                 dma(n_blk - 1),
                 dma(n_grp - 1),
@@ -445,7 +448,7 @@
             )
         )
         img, txt, bias = pl.pallas_call(
-            land,
+            functools.partial(land, 1.0 / count),
             out_shape=(
                 jax.ShapeDtypeStruct((size, ds), f32),
                 jax.ShapeDtypeStruct((size, ds), f32),
@@ -453,9 +456,9 @@
             ),
             in_specs=[pl.BlockSpec(memory_space=pltpu.VMEM)] * 3,
             out_specs=[pl.BlockSpec(memory_space=pl.ANY)] * 3,
-            scratch_shapes=[dma(3)],
+            scratch_shapes=[pltpu.VMEM((1, 1), f32), dma(3)],
             compiler_params=pltpu.CompilerParams(vmem_limit_bytes=30 * 1024 * 1024),
-        )(far, near, bias)
+        )(far, near, total)
         return img[None, None], txt[None, None], bias[0, 0]
 
     return jax.shard_map(

time: 59.4 us -> 53.8 us (0.906)
  Pallas kernels: 57.9 us -> 52.7 us
    pallas_call x2, Pallas kernels: 57.9 us -> 52.7 us  [the longest x1 51.6 us: body(): pl.pallas_call(functools.partial(kernel, n_blk, n_grp, ds), out_shape=(ja...]
where the time goes in v2:
time: 53.8 us; the launch traced here: 53.4 us
  Pallas kernels  52.7 us (98%)
  between operations  0.64 us (1%)
    pallas_call x1, Pallas kernels, body(): pl.pallas_call(functools.partial(kernel, n_blk, n_grp, ds), out_shape=(ja...  51.6 us
    pallas_call x1, Pallas kernels, body(): pl.pallas_call(functools.partial(land, 1.0 / count), out_shape=(jax.Shape...  1.18 us

profile of v2, /device:TPU:2, one launch (start us, length us, event | category | flops | bytes accessed | tf_op | source)
XLA Modules:
  0.0 53.4 jit_solution(3636772254644322853)
XLA Ops:
  0.6 51.6 %shard_map.76 = (f32[256,768]{1,0:T(8,128)S(1)}, f32[256,768]{1,0:T(8,128)S(1)}, f32[8,128]{1,0:T(8,128)S(1)}) custom-call(bf16[256,768]{1,0:T(8,128)(2,1)} %bitcast.10, bf16[256,1152]{1,0:T(8,128)(2,1)} %bitcast.8, bf16[256,768]{1,0:T(8,128)(2,1)} %bitcast.11, bf16[256,1152]{1,0:T(8,128)(2,1)} %bitcast.9, s32[1,256]{1,0:T(1,128)} %bitcast.12), custom_call_target="tpu_custom_call" | custom-call | tf_op jit(solution)/shard_map/pallas_call | solution.py:386
  52.2 1.2 %shard_map.77 = (f32[256,768]{1,0:T(8,128)}, f32[256,768]{1,0:T(8,128)}, f32[1,1]{1,0:T(1,128)}) custom-call(f32[256,768]{1,0:T(8,128)S(1)} %get-tuple-element.9.of_far, f32[256,768]{1,0:T(8,128)S(1)} %get-tuple-element.10.of_near, f32[8,128]{1,0:T(8,128)S(1)} %get-tuple-element.11.total), custom_call_target="tpu_custom_call" | custom-call | tf_op jit(solution)/shard_map/pallas_call | solution.py:450

commit v3 on v2

--- a/solution.py
+++ b/solution.py
@@ -10,8 +10,8 @@
 
 MESH = pl.DeviceIdType.MESH
 WINDOW = 4
-FAR = 2
-NEAR = 2
+FAR = (2, 2)
+NEAR = (9, 7)
 PLAIN = ("nnff", "")
 NEAR_WRAPS = ("ff", "nn")
 FAR_WRAPS = ("", "ffnn")
@@ -139,10 +139,22 @@
             device_id={"blk": b, "grp": lax.rem(g + k, n_grp)},
             device_id_type=MESH,
         )
+    pl.semaphore_wait(barrier, expected)
+
+    def tell(sem, offset):
+        pl.semaphore_signal(sem, inc=1, device_id=at_blk(b + offset), device_id_type=MESH)
+
+    @pl.when(jnp.logical_not(has_down))
+    def _():
+        tell(up_sem, 2)
+
+    @pl.when(jnp.logical_not(has_up))
+    def _():
+        tell(down_sem, -2)
+
     for c in loads(txt_stu, txt_tea, img_stu, img_tea):
         c.wait()
     ids_load.wait()
-    pl.semaphore_wait(barrier, expected)
 
     def remote(src, dst, send, recv, to):
         return pltpu.make_async_remote_copy(
@@ -150,8 +162,12 @@
             device_id=to, device_id_type=MESH,
         )
 
-    def pieces(n):
-        return [(pl.ds(i * (size // n), size // n), slice(i * (size // n), (i + 1) * (size // n))) for i in range(n)]
+    def pieces(parts):
+        unit, at, out = size // sum(parts), 0, []
+        for part in parts:
+            out.append((pl.ds(at, part * unit), slice(at, at + part * unit)))
+            at += part * unit
+        return out
 
     far_rows, near_rows = pieces(FAR), pieces(NEAR)
     ids_f = remote(own_ids, far_ids_in, ids_send.at[0], ids_recv.at[0], at_blk(far_to))
@@ -183,22 +199,24 @@
             sent[kind] += 1
 
     plain = jnp.logical_not(jnp.logical_or(near_wraps, far_wraps))
-    cases = ((plain, PLAIN), (near_wraps, NEAR_WRAPS), (far_wraps, FAR_WRAPS))
+    is_last = jnp.where(role == 0, b == n_blk - 1, b == 0)
+    cases = (
+        (plain, PLAIN), (near_wraps, NEAR_WRAPS),
+        (jnp.logical_and(far_wraps, jnp.logical_not(is_last)), FAR_WRAPS),
+        (jnp.logical_and(far_wraps, is_last), ('n', 'ffn')),
+    )
     for case, (at_once, _) in cases:
 
         @pl.when(case)
         def _():
             begin(at_once)
-
-    def tell(sem, offset):
-        pl.semaphore_signal(sem, inc=1, device_id=at_blk(b + offset), device_id_type=MESH)
 
     def pass_up():
         @pl.when(has_down)
         def _():
             pl.semaphore_wait(up_sem, 1)
 
-        @pl.when(has_up)
+        @pl.when(jnp.logical_and(has_down, has_up))
         def _():
             tell(up_sem, 2)
 
@@ -207,7 +225,7 @@
         def _():
             pl.semaphore_wait(down_sem, 1)
 
-        @pl.when(has_down)
+        @pl.when(jnp.logical_and(has_down, has_up))
         def _():
             tell(down_sem, -2)
 
@@ -305,11 +323,12 @@
             back = dot_nn(w1, e_own[:, :ds]) + dot_nn(w2, e_in[:, :ds])
             l_out[rows, :] = (back * scale_s).astype(jnp.bfloat16)
             l_back[i].start()
+            part[...] += dot_tn(w2, x[:, :ds])
+            if i == len(l_rows) - 1:
+                for c, (back_rows, _) in zip(e_back, e_rows):
+                    e_out[back_rows, :] = (part[back_rows, :] * scale_s).astype(jnp.bfloat16)
+                    c.start()
             e_acc[...] += dot_tn(w1, x[:, :ds])
-            part[...] += dot_tn(w2, x[:, :ds])
-        for i, (rows, _) in enumerate(e_rows):
-            e_out[rows, :] = (part[rows, :] * scale_s).astype(jnp.bfloat16)
-            e_back[i].start()
 
     process(far_side, near_side)
 
@@ -415,16 +434,16 @@
                 pltpu.VMEM((8, 128), f32),
                 pltpu.VMEM((n_grp, 8, 128), f32),
                 dma(5),
-                dma(FAR),
-                dma(FAR),
-                dma(NEAR),
-                dma(NEAR),
+                dma(len(FAR)),
+                dma(len(FAR)),
+                dma(len(NEAR)),
+                dma(len(NEAR)),
                 dma(2),
                 dma(2),
-                dma(FAR),
-                dma(FAR),
-                dma(NEAR),
-                dma(NEAR),
+                dma(len(FAR)),
+                dma(len(FAR)),
+                dma(len(NEAR)),
+                dma(len(NEAR)),
                 dma(n_blk - 1),
                 dma(n_blk - 1),
                 dma(n_grp - 1),

time: 53.8 us -> 53.5 us (level)
  no operation moved by 1% of the time
where the time goes in v3:
time: 53.5 us; the launch traced here: 53.4 us
  Pallas kernels  52.7 us (99%)
  between operations  0.64 us (1%)
    pallas_call x1, Pallas kernels, body(): pl.pallas_call(functools.partial(kernel, n_blk, n_grp, ds), out_shape=(ja...  51.6 us
    pallas_call x1, Pallas kernels, body(): pl.pallas_call(functools.partial(land, 1.0 / count), out_shape=(jax.Shape...  1.18 us

profile of v3, /device:TPU:2, one launch (start us, length us, event | category | flops | bytes accessed | tf_op | source)
XLA Modules:
  0.0 53.4 jit_solution(1387484079810445473)
XLA Ops:
  0.6 51.6 %shard_map.76 = (f32[256,768]{1,0:T(8,128)S(1)}, f32[256,768]{1,0:T(8,128)S(1)}, f32[8,128]{1,0:T(8,128)S(1)}) custom-call(bf16[256,768]{1,0:T(8,128)(2,1)} %bitcast.10, bf16[256,1152]{1,0:T(8,128)(2,1)} %bitcast.8, bf16[256,768]{1,0:T(8,128)(2,1)} %bitcast.11, bf16[256,1152]{1,0:T(8,128)(2,1)} %bitcast.9, s32[1,256]{1,0:T(1,128)} %bitcast.12), custom_call_target="tpu_custom_call" | custom-call | tf_op jit(solution)/shard_map/pallas_call | solution.py:405
  52.2 1.2 %shard_map.77 = (f32[256,768]{1,0:T(8,128)}, f32[256,768]{1,0:T(8,128)}, f32[1,1]{1,0:T(1,128)}) custom-call(f32[256,768]{1,0:T(8,128)S(1)} %get-tuple-element.9.of_far, f32[256,768]{1,0:T(8,128)S(1)} %get-tuple-element.10.of_near, f32[8,128]{1,0:T(8,128)S(1)} %get-tuple-element.11.total), custom_call_target="tpu_custom_call" | custom-call | tf_op jit(solution)/shard_map/pallas_call | solution.py:469

commit v4 on v2

--- a/solution.py
+++ b/solution.py
@@ -10,11 +10,11 @@
 
 MESH = pl.DeviceIdType.MESH
 WINDOW = 4
-FAR = 2
+FAR = 1
 NEAR = 2
-PLAIN = ("nnff", "")
-NEAR_WRAPS = ("ff", "nn")
-FAR_WRAPS = ("", "ffnn")
+PLAIN = ("nnf", "")
+NEAR_WRAPS = ("f", "nn")
+FAR_WRAPS = ("", "fnn")
 
 
 def dot_nt(a, b):

time: 53.8 us -> 53.6 us (level)
  no operation moved by 1% of the time
where the time goes in v4:
time: 53.6 us; the launch traced here: 53.4 us
  Pallas kernels  52.7 us (98%)
  between operations  0.64 us (1%)
    pallas_call x1, Pallas kernels, body(): pl.pallas_call(functools.partial(kernel, n_blk, n_grp, ds), out_shape=(ja...  51.6 us
    pallas_call x1, Pallas kernels, body(): pl.pallas_call(functools.partial(land, 1.0 / count), out_shape=(jax.Shape...  1.18 us

profile of v4, /device:TPU:2, one launch (start us, length us, event | category | flops | bytes accessed | tf_op | source)
XLA Modules:
  0.0 53.4 jit_solution(54118127744130338)
XLA Ops:
  0.6 51.6 %shard_map.76 = (f32[256,768]{1,0:T(8,128)S(1)}, f32[256,768]{1,0:T(8,128)S(1)}, f32[8,128]{1,0:T(8,128)S(1)}) custom-call(bf16[256,768]{1,0:T(8,128)(2,1)} %bitcast.10, bf16[256,1152]{1,0:T(8,128)(2,1)} %bitcast.8, bf16[256,768]{1,0:T(8,128)(2,1)} %bitcast.11, bf16[256,1152]{1,0:T(8,128)(2,1)} %bitcast.9, s32[1,256]{1,0:T(1,128)} %bitcast.12), custom_call_target="tpu_custom_call" | custom-call | tf_op jit(solution)/shard_map/pallas_call | solution.py:386
  52.2 1.2 %shard_map.77 = (f32[256,768]{1,0:T(8,128)}, f32[256,768]{1,0:T(8,128)}, f32[1,1]{1,0:T(1,128)}) custom-call(f32[256,768]{1,0:T(8,128)S(1)} %get-tuple-element.9.of_far, f32[256,768]{1,0:T(8,128)S(1)} %get-tuple-element.10.of_near, f32[8,128]{1,0:T(8,128)S(1)} %get-tuple-element.11.total), custom_call_target="tpu_custom_call" | custom-call | tf_op jit(solution)/shard_map/pallas_call | solution.py:450

commit v5 on v2

--- a/solution.py
+++ b/solution.py
@@ -15,6 +15,7 @@
 PLAIN = ("nnff", "")
 NEAR_WRAPS = ("ff", "nn")
 FAR_WRAPS = ("", "ffnn")
+LAST = ("nn", "ff")
 
 
 def dot_nt(a, b):
@@ -183,7 +184,13 @@
             sent[kind] += 1
 
     plain = jnp.logical_not(jnp.logical_or(near_wraps, far_wraps))
-    cases = ((plain, PLAIN), (near_wraps, NEAR_WRAPS), (far_wraps, FAR_WRAPS))
+    is_last = jnp.where(role == 0, b == n_blk - 1, b == 0)
+    cases = (
+        (plain, PLAIN),
+        (near_wraps, NEAR_WRAPS),
+        (jnp.logical_and(far_wraps, jnp.logical_not(is_last)), FAR_WRAPS),
+        (jnp.logical_and(far_wraps, is_last), LAST),
+    )
     for case, (at_once, _) in cases:
 
         @pl.when(case)

time: 53.8 us -> 53.8 us (level)
  no operation moved by 1% of the time
where the time goes in v5:
time: 53.8 us; the launch traced here: 53.4 us
  Pallas kernels  52.7 us (98%)
  between operations  0.64 us (1%)
    pallas_call x1, Pallas kernels, body(): pl.pallas_call(functools.partial(kernel, n_blk, n_grp, ds), out_shape=(ja...  51.6 us
    pallas_call x1, Pallas kernels, body(): pl.pallas_call(functools.partial(land, 1.0 / count), out_shape=(jax.Shape...  1.18 us

profile of v5, /device:TPU:2, one launch (start us, length us, event | category | flops | bytes accessed | tf_op | source)
XLA Modules:
  0.0 53.4 jit_solution(16049177533328911609)
XLA Ops:
  0.6 51.6 %shard_map.76 = (f32[256,768]{1,0:T(8,128)S(1)}, f32[256,768]{1,0:T(8,128)S(1)}, f32[8,128]{1,0:T(8,128)S(1)}) custom-call(bf16[256,768]{1,0:T(8,128)(2,1)} %bitcast.10, bf16[256,1152]{1,0:T(8,128)(2,1)} %bitcast.8, bf16[256,768]{1,0:T(8,128)(2,1)} %bitcast.11, bf16[256,1152]{1,0:T(8,128)(2,1)} %bitcast.9, s32[1,256]{1,0:T(1,128)} %bitcast.12), custom_call_target="tpu_custom_call" | custom-call | tf_op jit(solution)/shard_map/pallas_call | solution.py:393
  52.2 1.2 %shard_map.77 = (f32[256,768]{1,0:T(8,128)}, f32[256,768]{1,0:T(8,128)}, f32[1,1]{1,0:T(1,128)}) custom-call(f32[256,768]{1,0:T(8,128)S(1)} %get-tuple-element.9.of_far, f32[256,768]{1,0:T(8,128)S(1)} %get-tuple-element.10.of_near, f32[8,128]{1,0:T(8,128)S(1)} %get-tuple-element.11.total), custom_call_target="tpu_custom_call" | custom-call | tf_op jit(solution)/shard_map/pallas_call | solution.py:457
